TPU v7x, 32 devices: a whole 2x2x4 slice. The times are simulated.
32 devices in a mesh: head: 2 (over core), seq: 16 (over z, y, x).
Axes of the slice: x: 2, y: 2, z: 4, core: 2. Of those that a mesh axis runs over, the one named last changes fastest.
Arguments:
- queries: bfloat16 [8192, 5120], P(('seq', 'head')), may hold values from -8 to 8
- key_states: bfloat16 [8192, 5120], P(('seq', 'head')), may hold values from -8 to 8
- value_states: bfloat16 [8192, 5120], P(('seq', 'head')), may hold values from -6 to 6
- cluster_perm: int32 [40, 8192], P('head', 'seq'), may hold values from 0 to 8191, as said below
- block_mask: int32 [40, 64, 64], P('head', 'seq'), may hold values from 0 to 1, as said below
Outputs:
- attention_out: bfloat16 [8192, 5120], P(('seq', 'head'))
Inputs may be any that keep to these rules, and one draw needn't show every extreme that they name: `cluster_perm`: for each head, positions k * 512 to (k + 1) * 512 - 1 list the tokens k * 512 to (k + 1) * 512 - 1, each once. `block_mask`: for each head and each aligned run of 4 query blocks, the key blocks used by some query block of the run number exactly 1. For such a run and the 20 heads g * 20 to (g + 1) * 20 - 1, the (head, key block) pairs so used that lie in one aligned run of 4 key blocks number at most 2, and exactly 2 in some run. Every query block uses 1 to 1 key blocks, and some query block of every run uses 1, for every head.
All inputs are finite; a program needn't handle non-finite values.
Results may differ from a plain program's by a relative error of at most 0.0049.
Values may be sent and summed in bfloat16 or wider, within the bound.
A program may use at most 128 MiB of HBM per device.

v0:
```python
import math
import jax
import jax.numpy as jnp
from jax import lax
from jax.sharding import PartitionSpec as P

HEAD_DIM = 128
BLOCK = 128


def shards(queries, key_states, value_states, cluster_perm, block_mask):
    group_heads = cluster_perm.shape[0]
    shard_rows = cluster_perm.shape[1]
    shard_blocks = shard_rows // BLOCK
    seq_count = lax.axis_size("seq")
    block_total = block_mask.shape[2]
    pick_count = max(1, block_total // 64)
    live_most = min(5, pick_count)
    capacity = max(
        1, min(shard_blocks, (group_heads * pick_count * 8 + 5 * seq_count - 1) // (5 * seq_count))
    )
    pair_count = group_heads * shard_blocks
    slot_total = seq_count * capacity
    score_scale = 1.0 / math.sqrt(HEAD_DIM)
    query_rows, key_rows, value_rows = (
        lax.all_to_all(queries, "head", split_axis=1, concat_axis=0, tiled=True),
        lax.all_to_all(key_states, "head", split_axis=1, concat_axis=0, tiled=True),
        lax.all_to_all(value_states, "head", split_axis=1, concat_axis=0, tiled=True),
    )
    local_perm = cluster_perm - lax.axis_index("seq") * shard_rows
    row_ids = jnp.arange(shard_rows, dtype=jnp.int32)
    order_table = (local_perm[:, :, None] == row_ids[None, None, :]).astype(jnp.bfloat16)
    stacked = jnp.concatenate(
        [
            query_rows.reshape(shard_rows, group_heads, HEAD_DIM),
            key_rows.reshape(shard_rows, group_heads, HEAD_DIM),
            value_rows.reshape(shard_rows, group_heads, HEAD_DIM),
        ],
        axis=2,
    )
    sorted_all = jnp.einsum(
        "hit,thd->hid", order_table, stacked, preferred_element_type=jnp.float32
    ).astype(jnp.bfloat16)
    query_sorted = sorted_all[:, :, :HEAD_DIM]
    key_sorted = sorted_all[:, :, HEAD_DIM : 2 * HEAD_DIM]
    value_sorted = sorted_all[:, :, 2 * HEAD_DIM :]
    needed = jnp.max(block_mask, axis=1)
    by_owner = needed.reshape(group_heads, seq_count, shard_blocks)
    requested = lax.all_to_all(by_owner, "seq", split_axis=1, concat_axis=1, tiled=True)

    def slot_ranks(bit_table):
        flat_bits = bit_table.transpose(1, 0, 2).reshape(seq_count, pair_count)
        return (flat_bits, jnp.cumsum(flat_bits, axis=1) - flat_bits)

    asked_bits, asked_rank = slot_ranks(requested)
    cap_ids = jnp.arange(capacity, dtype=jnp.int32)
    matches = (asked_bits[:, :, None] == 1) & (asked_rank[:, :, None] == cap_ids[None, None, :])
    send_table = matches.transpose(0, 2, 1).astype(jnp.bfloat16)
    block_width = BLOCK * HEAD_DIM
    kv_pairs = jnp.concatenate(
        [
            key_sorted.reshape(pair_count, block_width),
            value_sorted.reshape(pair_count, block_width),
        ],
        axis=1,
    )
    kv_send = jnp.einsum(
        "scp,pw->scw", send_table, kv_pairs, preferred_element_type=jnp.float32
    ).astype(jnp.bfloat16)
    key_send = kv_send[:, :, :block_width].reshape(seq_count, capacity, BLOCK, HEAD_DIM)
    value_send = kv_send[:, :, block_width:].reshape(seq_count, capacity, BLOCK, HEAD_DIM)
    own_bits, own_rank = slot_ranks(by_owner)
    prefix = jnp.cumsum(needed, axis=1) - needed
    chosen = (needed[:, :, None] == 1) & (
        prefix[:, :, None] == jnp.arange(pick_count, dtype=jnp.int32)[None, None, :]
    )
    picked = jnp.sum(
        jnp.where(chosen, jnp.arange(block_total, dtype=jnp.int32)[None, :, None], 0), axis=1
    )
    owner_idx = picked // shard_blocks
    pair_idx = (
        jnp.arange(group_heads, dtype=jnp.int32)[:, None] * shard_blocks + picked % shard_blocks
    )
    slot_idx = jnp.take(own_rank.reshape(-1), owner_idx * pair_count + pair_idx)
    position = owner_idx * capacity + slot_idx
    live_bits = jnp.take_along_axis(block_mask, picked[:, None, :], axis=2)
    query_blocks = query_sorted.reshape(group_heads, shard_blocks, BLOCK, HEAD_DIM)
    rank_live = jnp.cumsum(live_bits, axis=2) - live_bits
    selected = (live_bits[..., None] == 1) & (
        rank_live[..., None] == jnp.arange(live_most, dtype=jnp.int32)
    )
    which_pick = jnp.sum(
        jnp.where(selected, jnp.arange(pick_count, dtype=jnp.int32)[None, None, :, None], 0), axis=2
    )
    usable = jnp.any(selected, axis=2)
    key_pos = jnp.take_along_axis(
        jnp.broadcast_to(position[:, None, :], live_bits.shape), which_pick, axis=2
    )
    score_form = "qid,qljd->qilj"
    mix_form = "qilj,qljd->qid"
    slot_ids = jnp.arange(slot_total, dtype=jnp.int32)

    def select_blocks(got_flat, slot_head):
        pick_table = (slot_head[..., None] == slot_ids).astype(jnp.bfloat16)
        chosen_rows = jnp.einsum(
            "...s,sw->...w", pick_table, got_flat, preferred_element_type=jnp.float32
        ).astype(jnp.bfloat16)
        return chosen_rows.reshape(slot_head.shape + (BLOCK, HEAD_DIM))

    def head_scores(query_head, key_got, slot_head, usable_head):
        key_sel = select_blocks(key_got, slot_head)
        scores = (
            jnp.einsum(score_form, query_head, key_sel, preferred_element_type=jnp.float32)
            * score_scale
        )
        return jnp.where(usable_head[:, None, :, None], scores, -jnp.inf)

    def head_mix(weights, value_got, slot_head):
        value_sel = select_blocks(value_got, slot_head)
        return jnp.einsum(mix_form, weights, value_sel, preferred_element_type=jnp.float32).astype(
            jnp.bfloat16
        )

    flat_shape = (slot_total, block_width)
    key_got, value_got = (
        lax.all_to_all(key_send, "seq", split_axis=0, concat_axis=0, tiled=True),
        lax.all_to_all(value_send, "seq", split_axis=0, concat_axis=0, tiled=True),
    )
    key_got = key_got.reshape(flat_shape)
    value_got = value_got.reshape(flat_shape)

    def full_pass(operands):
        query_head, slot_head, usable_head = operands
        scores = head_scores(query_head, key_got, slot_head, usable_head)
        row_top = jnp.max(scores, axis=(2, 3), keepdims=True)
        exponent = jnp.exp(scores - row_top)
        row_total = jnp.sum(exponent, axis=(2, 3), keepdims=True)
        weights = (exponent / row_total).astype(jnp.bfloat16)
        return head_mix(weights, value_got, slot_head)

    attended = lax.map(full_pass, (query_blocks, key_pos, usable))
    attended_flat = attended.reshape(group_heads, shard_rows, HEAD_DIM)
    restored = jnp.einsum(
        "hit,hid->thd", order_table, attended_flat, preferred_element_type=jnp.float32
    ).astype(jnp.bfloat16)
    out_rows = restored.reshape(shard_rows, group_heads * HEAD_DIM)
    return lax.all_to_all(out_rows, "head", split_axis=0, concat_axis=1, tiled=True)


def solution(mesh):
    placed = (
        P(("seq", "head"), None),
        P(("seq", "head"), None),
        P(("seq", "head"), None),
        P("head", "seq"),
        P("head", "seq", None),
    )
    return jax.shard_map(
        shards, mesh=mesh, in_specs=placed, out_specs=P(("seq", "head"), None), check_vma=False
    )
```

profile of v0, /device:TPU:9, one launch (start us, length us, event | category | flops | bytes accessed | tf_op | source)
XLA Modules:
  0.0 287.1 jit_solution(12030051631349020649)
XLA Ops:
  0.0 4.4 %copy.43 = bf16[256,5120]{0,1:T(8,128)(2,1)} copy(bf16[256,5120]{1,0:T(8,128)(2,1)} %param.7) | data formatting | bytes 5242880 | tf_op args[0]
  4.4 4.7 %all-to-all-start = ((bf16[256,2,2560]{0,2,1:T(8,128)(2,1)}), bf16[256,2,2560]{0,2,1:T(8,128)(2,1)S(1)}, u32[]{:S(2)}, u32[]{:S(2)}) async-start(bf16[256,2,2560]{0,2,1:T(8,128)(2,1)} %bitcast.147), calls=%async_computation | async-start | bytes 5242880 | tf_op jit(solution)/shard_map/all_to_all | solution.py:26
  9.8 4.4 %copy.45 = bf16[256,5120]{0,1:T(8,128)(2,1)} copy(bf16[256,5120]{1,0:T(8,128)(2,1)} %param.8) | data formatting | bytes 5242880 | tf_op args[1]
  14.2 5.0 %all-to-all-start.1 = ((bf16[256,2,2560]{0,2,1:T(8,128)(2,1)}), bf16[256,2,2560]{0,2,1:T(8,128)(2,1)}, u32[]{:S(2)}, u32[]{:S(2)}) async-start(bf16[256,2,2560]{0,2,1:T(8,128)(2,1)} %bitcast.145), calls=%async_computation.1 | async-start | bytes 5242880 | tf_op jit(solution)/shard_map/all_to_all | solution.py:27
  19.2 17.3 %copy.44 = bf16[2,256,2560]{1,0,2:T(2,128)(2,1)} copy(bf16[2,256,2560]{1,2,0:T(8,128)(2,1)S(1)} %bitcast.143) | data formatting | bytes 5242880 | tf_op jit(solution)/shard_map/all_to_all | solution.py:26
  36.5 4.2 %reshape.468 = bf16[512,20,128]{0,2,1:T(8,128)(2,1)S(1)} reshape(bf16[2,256,2560]{1,0,2:T(2,128)(2,1)} %copy.44) | data formatting | bytes 5242880 | tf_op jit(solution)/shard_map/reshape | solution.py:35
  40.7 2.6 copy.49
  43.2 4.4 %copy.47 = bf16[256,5120]{0,1:T(8,128)(2,1)} copy(bf16[256,5120]{1,0:T(8,128)(2,1)} %param.9) | data formatting | bytes 5242880 | tf_op args[2]
  47.6 3.9 %all-to-all-start.2 = ((bf16[256,2,2560]{0,2,1:T(8,128)(2,1)}), bf16[256,2,2560]{0,2,1:T(8,128)(2,1)S(1)}, u32[]{:S(2)}, u32[]{:S(2)}) async-start(bf16[256,2,2560]{0,2,1:T(8,128)(2,1)} %bitcast.146), calls=%async_computation.2 | async-start | bytes 5242880 | tf_op jit(solution)/shard_map/all_to_all | solution.py:28
  51.5 7.0 %copy.46 = bf16[2,256,2560]{1,0,2:T(2,128)(2,1)} copy(bf16[2,256,2560]{1,2,0:T(8,128)(2,1)} %bitcast.7) | data formatting | bytes 5242880 | tf_op jit(solution)/shard_map/all_to_all | solution.py:27
  58.4 5.4 %reshape.469 = bf16[512,20,128]{0,2,1:T(8,128)(2,1)} reshape(bf16[2,256,2560]{1,0,2:T(2,128)(2,1)} %copy.46) | data formatting | bytes 5242880 | tf_op jit(solution)/shard_map/reshape | solution.py:36
  63.8 4.4 %copy.50 = bf16[512,20,128]{2,0,1:T(8,128)(2,1)} copy(bf16[512,20,128]{0,2,1:T(8,128)(2,1)} %reshape.469) | data formatting | bytes 5242880 | tf_op jit(solution)/shard_map/reshape | solution.py:36
  68.2 6.7 %all-to-all-start.3 = ((s32[20,16,4]{0,2,1:T(4,128)}), s32[20,16,4]{0,2,1:T(4,128)S(1)}, u32[]{:S(2)}, u32[]{:S(2)}) async-start(s32[20,16,4]{0,2,1:T(4,128)} %bitcast.11), calls=%async_computation.3 | async-start | bytes 65536 | tf_op jit(solution)/shard_map/all_to_all | solution.py:49
  74.9 17.3 %copy.48 = bf16[2,256,2560]{1,0,2:T(2,128)(2,1)} copy(bf16[2,256,2560]{1,2,0:T(8,128)(2,1)S(1)} %bitcast.144) | data formatting | bytes 5242880 | tf_op jit(solution)/shard_map/all_to_all | solution.py:28
  92.2 4.2 %reshape.470 = bf16[512,20,128]{0,2,1:T(8,128)(2,1)S(1)} reshape(bf16[2,256,2560]{1,0,2:T(2,128)(2,1)} %copy.48) | data formatting | bytes 5242880 | tf_op jit(solution)/shard_map/reshape | solution.py:37
  96.3 2.6 copy.51
  98.9 7.9 %fusion.39 = bf16[20,512,384]{2,1,0:T(8,128)(2,1)S(1)} fusion(bf16[512,20,128]{2,0,1:T(8,128)(2,1)} %copy.51, bf16[512,20,128]{2,0,1:T(8,128)(2,1)} %copy.50, bf16[512,20,128]{2,0,1:T(8,128)(2,1)} %copy.49, s32[20,512]{1,0:T(8,128)S(1)} %broadcast_subtract_fusion), kind=kOutput, calls=%fused_computation.46 | convolution fusion | flops 4059299840 | bytes 15769600 | tf_op jit(solution)/shard_map/hit,thd->hid/dot_general | solution.py:41
  106.8 3.1 %fusion.68 = (bf16[20,512,128]{2,1,0:T(8,128)(2,1)}, bf16[20,512,128]{2,1,0:T(8,128)(2,1)S(1)}, bf16[20,512,128]{2,1,0:T(8,128)(2,1)}) fusion(bf16[20,512,384]{2,1,0:T(8,128)(2,1)S(1)} %fusion.39), kind=kLoop, calls=%fused_computation.102 | loop fusion | bytes 15728640 | tf_op jit(solution)/shard_map/slice | solution.py:45
  109.9 5.2 %reshape.475 = bf16[80,16384]{1,0:T(8,128)(2,1)} reshape(bf16[20,512,128]{2,1,0:T(8,128)(2,1)} %get-tuple-element.99) | data formatting | bytes 5242880 | tf_op jit(solution)/shard_map/reshape | solution.py:62
  115.1 3.1 %reshape.476 = bf16[80,16384]{1,0:T(8,128)(2,1)} reshape(bf16[20,512,128]{2,1,0:T(8,128)(2,1)S(1)} %get-tuple-element.100) | data formatting | bytes 5242880 | tf_op jit(solution)/shard_map/reshape | solution.py:63
  118.7 3.4 %convolution_convert_fusion.3 = bf16[16,2,32768]{2,0,1:T(8,128)(2,1)S(1)} fusion(bf16[80,16384]{1,0:T(8,128)(2,1)} %reshape.476, bf16[80,16384]{1,0:T(8,128)(2,1)} %reshape.475, s32[16,80]{1,0:T(8,128)S(1)} %sub.46, pred[16,80]{1,0:T(8,128)(4,1)S(1)} %copy.58), kind=kOutput, calls=%fused_computation.35 | convolution fusion | flops 179311616 | bytes 7346432 | tf_op jit(solution)/shard_map/scp,pw->scw/dot_general | solution.py:67
  123.5 6.4 %all-to-all-start.4 = ((bf16[16,2,128,128]{3,2,1,0:T(8,128)(2,1)}), bf16[16,2,128,128]{3,2,1,0:T(8,128)(2,1)S(1)}, u32[]{:S(2)}, u32[]{:S(2)}) async-start(bf16[16,2,128,128]{3,2,1,0:T(8,128)(2,1)} %copy.61), calls=%async_computation.4 | async-start | bytes 2097152 | tf_op jit(solution)/shard_map/all_to_all | solution.py:126
  131.1 23.1 %all-to-all-done.4 = bf16[16,2,128,128]{3,2,1,0:T(8,128)(2,1)S(1)} async-done(((bf16[16,2,128,128]{3,2,1,0:T(8,128)(2,1)}), bf16[16,2,128,128]{3,2,1,0:T(8,128)(2,1)S(1)}, u32[]{:S(2)}, u32[]{:S(2)}) %all-to-all-start.4) | async-done | bytes 1048608 | tf_op jit(solution)/shard_map/all_to_all | solution.py:126
  154.2 4.5 %all-to-all-start.5 = ((bf16[16,2,128,128]{3,2,1,0:T(8,128)(2,1)}), bf16[16,2,128,128]{3,2,1,0:T(8,128)(2,1)S(1)}, u32[]{:S(2)}, u32[]{:S(2)}) async-start(bf16[16,2,128,128]{3,2,1,0:T(8,128)(2,1)} %copy.62), calls=%async_computation.5 | async-start | bytes 2097152 | tf_op jit(solution)/shard_map/all_to_all | solution.py:127
  162.9 1.8 gather_fusion.2
  166.4 16.7 %all-to-all-done.5 = bf16[16,2,128,128]{3,2,1,0:T(8,128)(2,1)S(1)} async-done(((bf16[16,2,128,128]{3,2,1,0:T(8,128)(2,1)}), bf16[16,2,128,128]{3,2,1,0:T(8,128)(2,1)S(1)}, u32[]{:S(2)}, u32[]{:S(2)}) %all-to-all-start.5) | async-done | bytes 1048608 | tf_op jit(solution)/shard_map/all_to_all | solution.py:127
  183.8 81.5 %while.11 = (s32[]{:T(128)}, bf16[20,4,128,128]{3,2,1,0:T(8,128)(2,1)}, pred[20,4,1]{0,1,2:T(4,128)(4,1)S(1)}, bf16[20,4,128,128]{3,2,1,0:T(8,128)(2,1)}, s32[20...) while((s32[]{:T(128)}, ...), condition=%wide.region_8.9_spmd.clone, body=%wide.region_5.8_spmd.clone.sunk | while | flops 59507712 | bytes 3936457 | solution.py:141
  184.4 1.2 fusion.99
  265.4 7.2 %convert_bitcast_fusion = bf16[512,20,128]{0,2,1:T(8,128)(2,1)} fusion(bf16[20,512,128]{2,1,0:T(8,128)(2,1)} %bitcast.162, s32[20,512]{1,0:T(8,128)S(1)} %broadcast_subtract_fusion), kind=kOutput, calls=%fused_computation.50 | convolution fusion | flops 1348730880 | bytes 5283840 | tf_op jit(solution)/shard_map/hit,hid->thd/dot_general | solution.py:143
  272.6 3.5 %all_to_all.71 = bf16[2,256,2560]{1,0,2:T(2,128)(2,1)S(1)} reshape(bf16[512,20,128]{0,2,1:T(8,128)(2,1)} %convert_bitcast_fusion) | data formatting | bytes 5242880 | tf_op jit(solution)/shard_map/all_to_all | solution.py:147
  276.5 7.9 %all_to_all.82 = bf16[2,256,2560]{1,2,0:T(8,128)(2,1)S(1)} all-to-all(bf16[2,256,2560]{1,2,0:T(8,128)(2,1)S(1)} %copy.66), channel_id=1, replica_groups=mesh['head'=2,'seq'=16] {'head'}, dimensions={0} | all-to-all | bytes 5242880 | tf_op jit(solution)/shard_map/all_to_all | solution.py:147
  284.4 2.8 copy.67
  (215 shorter events, 90.8 us)
Async XLA Ops:
  4.4 4.7 %copy-start = (s32[20,4,64]{2,1,0:T(4,128)S(1)}, s32[20,4,64]{2,1,0:T(4,128)}, u32[]{:S(2)}) copy-start(s32[20,4,64]{2,1,0:T(4,128)} %param.11) | copy-start | bytes 61444
  4.4 9.8 %all-to-all-start = ((bf16[256,2,2560]{0,2,1:T(8,128)(2,1)}), bf16[256,2,2560]{0,2,1:T(8,128)(2,1)S(1)}, u32[]{:S(2)}, u32[]{:S(2)}) async-start(bf16[256,2,2560]{0,2,1:T(8,128)(2,1)} %bitcast.147), calls=%async_computation | async-start | bytes 5242880 | tf_op jit(solution)/shard_map/all_to_all | solution.py:26
  14.2 33.4 %all-to-all-start.1 = ((bf16[256,2,2560]{0,2,1:T(8,128)(2,1)}), bf16[256,2,2560]{0,2,1:T(8,128)(2,1)}, u32[]{:S(2)}, u32[]{:S(2)}) async-start(bf16[256,2,2560]{0,2,1:T(8,128)(2,1)} %bitcast.145), calls=%async_computation.1 | async-start | bytes 5242880 | tf_op jit(solution)/shard_map/all_to_all | solution.py:27
  47.6 20.6 %all-to-all-start.2 = ((bf16[256,2,2560]{0,2,1:T(8,128)(2,1)}), bf16[256,2,2560]{0,2,1:T(8,128)(2,1)S(1)}, u32[]{:S(2)}, u32[]{:S(2)}) async-start(bf16[256,2,2560]{0,2,1:T(8,128)(2,1)} %bitcast.146), calls=%async_computation.2 | async-start | bytes 5242880 | tf_op jit(solution)/shard_map/all_to_all | solution.py:28
  68.2 49.9 %all-to-all-start.3 = ((s32[20,16,4]{0,2,1:T(4,128)}), s32[20,16,4]{0,2,1:T(4,128)S(1)}, u32[]{:S(2)}, u32[]{:S(2)}) async-start(s32[20,16,4]{0,2,1:T(4,128)} %bitcast.11), calls=%async_computation.3 | async-start | bytes 65536 | tf_op jit(solution)/shard_map/all_to_all | solution.py:49
  96.3 2.6 copy-start.1
  123.5 30.7 %all-to-all-start.4 = ((bf16[16,2,128,128]{3,2,1,0:T(8,128)(2,1)}), bf16[16,2,128,128]{3,2,1,0:T(8,128)(2,1)S(1)}, u32[]{:S(2)}, u32[]{:S(2)}) async-start(bf16[16,2,128,128]{3,2,1,0:T(8,128)(2,1)} %copy.61), calls=%async_computation.4 | async-start | bytes 2097152 | tf_op jit(solution)/shard_map/all_to_all | solution.py:126
  154.2 28.9 %all-to-all-start.5 = ((bf16[16,2,128,128]{3,2,1,0:T(8,128)(2,1)}), bf16[16,2,128,128]{3,2,1,0:T(8,128)(2,1)S(1)}, u32[]{:S(2)}, u32[]{:S(2)}) async-start(bf16[16,2,128,128]{3,2,1,0:T(8,128)(2,1)} %copy.62), calls=%async_computation.5 | async-start | bytes 2097152 | tf_op jit(solution)/shard_map/all_to_all | solution.py:127
where the time goes:
time: 290 us; the launch traced here: 287 us
  local copies, waits for them, and re-layouts  111 us (38%)
  matrix products  95.6 us (33%)
  waiting for transfers between devices  39.8 us (14%)
  starting transfers between devices  31.2 us (11%)
  blocking collectives  7.86 us (3%)
    sub x20, matrix products, full_pass(): exponent = jnp.exp(scores - row_top)  23.4 us
    all_to_all x1, waiting for transfers between devices, shards(): lax.all_to_all(key_send, 'seq', split_axis=0, concat_axis=0, tiled=True)  23.1 us
    dot_general x20, matrix products, head_scores(): jnp.einsum(score_form, query_head, key_sel, preferred_element_type=jnp.fl...  22.3 us
    dot_general x20, matrix products, head_mix(): jnp.einsum(mix_form, weights, value_sel, preferred_element_type=jnp.float32)  18.7 us
    all_to_all x1, local copies, waits for them, and re-layouts, shards(): lax.all_to_all(value_states, 'head', split_axis=1, concat_axis=0, tiled=T...  17.3 us
    all_to_all x1, local copies, waits for them, and re-layouts, shards(): lax.all_to_all(queries, 'head', split_axis=1, concat_axis=0, tiled=True)  17.3 us
    all_to_all x1, waiting for transfers between devices, shards(): lax.all_to_all(value_send, 'seq', split_axis=0, concat_axis=0, tiled=True)  16.7 us
    unnamed x15, local copies, waits for them, and re-layouts  15.3 us
  transfers between devices with their start and end apart: 6, of which 2 were waited for; matrix products, arithmetic and copies ran while one was open for 36% of the time, Pallas kernels for 0%

commit v1 on v0

--- a/solution.py
+++ b/solution.py
@@ -6,6 +6,13 @@
 
 HEAD_DIM = 128
 BLOCK = 128
+
+
+def exchange_blocks(x, mesh_axis, split, join):
+    size = lax.axis_size(mesh_axis)
+    blocks = jnp.stack(jnp.split(x, size, axis=split), axis=0)
+    blocks = lax.all_to_all(blocks, mesh_axis, split_axis=0, concat_axis=0)
+    return jnp.concatenate(blocks, axis=join)
 
 
 def shards(queries, key_states, value_states, cluster_perm, block_mask):
@@ -23,7 +30,7 @@
     slot_total = seq_count * capacity
     score_scale = 1.0 / math.sqrt(HEAD_DIM)
     query_rows, key_rows, value_rows = (
-        lax.all_to_all(queries, "head", split_axis=1, concat_axis=0, tiled=True),
+        exchange_blocks(queries, "head", 1, 0),
         lax.all_to_all(key_states, "head", split_axis=1, concat_axis=0, tiled=True),
         lax.all_to_all(value_states, "head", split_axis=1, concat_axis=0, tiled=True),
     )

time: 290 us -> 272 us (0.938)
  local copies, waits for them, and re-layouts: 111 us -> 92.4 us
    all_to_all x1 -> x0, local copies, waits for them, and re-layouts: 17.3 us -> none  [shards(): lax.all_to_all(queries, 'head', split_axis=1, concat_axis=0, tiled=True)]
    another operation x0 -> x3, local copies, waits for them, and re-layouts: none -> 8.13 us  [the longest x2 6.25 us: shards(): query_rows.reshape(shard_rows, group_heads, HEAD_DIM)]
    reshape x2 -> x0, local copies, waits for them, and re-layouts: 6.74 us -> none  [shards(): query_rows.reshape(shard_rows, group_heads, HEAD_DIM)]
    all_to_all x1, waiting for transfers between devices: 16.7 us -> 23.1 us  [shards(): lax.all_to_all(value_send, 'seq', split_axis=0, concat_axis=0, tiled=True)]
    all_to_all x1, waiting for transfers between devices: 23.1 us -> 16.7 us  [shards(): lax.all_to_all(key_send, 'seq', split_axis=0, concat_axis=0, tiled=True)]
    unnamed x15 -> x16, local copies, waits for them, and re-layouts: 15.3 us -> 12.4 us
  transfers between devices with their start and end apart: 6 -> 6, of which waited for: 2 -> 2; matrix products, arithmetic and copies ran while one was open for 36% -> 31% of each run, Pallas kernels for 0% -> 0%
where the time goes in v1:
time: 272 us; the launch traced here: 270 us
  matrix products  95.6 us (35%)
  local copies, waits for them, and re-layouts  92.4 us (34%)
  waiting for transfers between devices  39.8 us (15%)
  starting transfers between devices  31.1 us (11%)
  blocking collectives  7.86 us (3%)
  other arithmetic  2.78 us (1%)
    sub x20, matrix products, full_pass(): exponent = jnp.exp(scores - row_top)  23.4 us
    all_to_all x1, waiting for transfers between devices, shards(): lax.all_to_all(value_send, 'seq', split_axis=0, concat_axis=0, tiled=True)  23.1 us
    dot_general x20, matrix products, head_scores(): jnp.einsum(score_form, query_head, key_sel, preferred_element_type=jnp.fl...  22.2 us
    dot_general x20, matrix products, head_mix(): jnp.einsum(mix_form, weights, value_sel, preferred_element_type=jnp.float32)  18.7 us
    all_to_all x1, local copies, waits for them, and re-layouts, shards(): lax.all_to_all(value_states, 'head', split_axis=1, concat_axis=0, tiled=T...  17.3 us
    all_to_all x1, waiting for transfers between devices, shards(): lax.all_to_all(key_send, 'seq', split_axis=0, concat_axis=0, tiled=True)  16.7 us
    dot_general x40, matrix products, select_blocks(): jnp.einsum('...s,sw->...w', pick_table, got_flat, preferred_element_type=...  12.8 us
    unnamed x16, local copies, waits for them, and re-layouts  12.4 us
  transfers between devices with their start and end apart: 6, of which 2 were waited for; matrix products, arithmetic and copies ran while one was open for 31% of the time, Pallas kernels for 0%

profile of v1, /device:TPU:9, one launch (start us, length us, event | category | flops | bytes accessed | tf_op | source)
XLA Modules:
  0.0 270.1 jit_solution(4986914976146314200)
XLA Ops:
  0.0 1.9 slice_bitcast_fusion.1
  1.9 1.7 pad_maximum_fusion
  3.6 4.7 %all-to-all-start = ((bf16[2,256,2560]{2,1,0:T(8,128)(2,1)}), bf16[2,256,2560]{2,1,0:T(8,128)(2,1)S(1)}, u32[]{:S(2)}, u32[]{:S(2)}) async-start(bf16[2,256,2560]{2,1,0:T(8,128)(2,1)} %pad_maximum_fusion), calls=%async_computation | async-start | bytes 5242880 | tf_op jit(solution)/shard_map/all_to_all | solution.py:14
  9.0 4.4 %copy.44 = bf16[256,5120]{0,1:T(8,128)(2,1)} copy(bf16[256,5120]{1,0:T(8,128)(2,1)} %param.8) | data formatting | bytes 5242880 | tf_op args[1]
  13.4 1.5 copy-done
  14.9 5.0 %all-to-all-start.1 = ((bf16[256,2,2560]{0,2,1:T(8,128)(2,1)}), bf16[256,2,2560]{0,2,1:T(8,128)(2,1)}, u32[]{:S(2)}, u32[]{:S(2)}) async-start(bf16[256,2,2560]{0,2,1:T(8,128)(2,1)} %bitcast.144), calls=%async_computation.1 | async-start | bytes 5242880 | tf_op jit(solution)/shard_map/all_to_all | solution.py:34
  19.9 4.2 %reshape.503 = bf16[512,20,128]{2,1,0:T(8,128)(2,1)S(1)} reshape(bf16[2,256,2560]{2,1,0:T(8,128)(2,1)} %copy-done) | data formatting | bytes 5242880 | tf_op jit(solution)/shard_map/reshape;reshape | solution.py:42
  24.1 2.1 copy.48
  26.2 4.4 %copy.46 = bf16[256,5120]{0,1:T(8,128)(2,1)} copy(bf16[256,5120]{1,0:T(8,128)(2,1)} %param.9) | data formatting | bytes 5242880 | tf_op args[2]
  30.6 3.9 %all-to-all-start.2 = ((bf16[256,2,2560]{0,2,1:T(8,128)(2,1)}), bf16[256,2,2560]{0,2,1:T(8,128)(2,1)S(1)}, u32[]{:S(2)}, u32[]{:S(2)}) async-start(bf16[256,2,2560]{0,2,1:T(8,128)(2,1)} %bitcast.145), calls=%async_computation.2 | async-start | bytes 5242880 | tf_op jit(solution)/shard_map/all_to_all | solution.py:35
  34.4 7.0 %copy.45 = bf16[2,256,2560]{1,0,2:T(2,128)(2,1)} copy(bf16[2,256,2560]{1,2,0:T(8,128)(2,1)} %bitcast.7) | data formatting | bytes 5242880 | tf_op jit(solution)/shard_map/all_to_all | solution.py:34
  41.4 5.4 %reshape.461 = bf16[512,20,128]{0,2,1:T(8,128)(2,1)} reshape(bf16[2,256,2560]{1,0,2:T(2,128)(2,1)} %copy.45) | data formatting | bytes 5242880 | tf_op jit(solution)/shard_map/reshape | solution.py:43
  46.8 4.4 %copy.49 = bf16[512,20,128]{2,0,1:T(8,128)(2,1)} copy(bf16[512,20,128]{0,2,1:T(8,128)(2,1)} %reshape.461) | data formatting | bytes 5242880 | tf_op jit(solution)/shard_map/reshape | solution.py:43
  51.2 6.7 %all-to-all-start.3 = ((s32[20,16,4]{0,2,1:T(4,128)}), s32[20,16,4]{0,2,1:T(4,128)S(1)}, u32[]{:S(2)}, u32[]{:S(2)}) async-start(s32[20,16,4]{0,2,1:T(4,128)} %bitcast.11), calls=%async_computation.3 | async-start | bytes 65536 | tf_op jit(solution)/shard_map/all_to_all | solution.py:56
  57.8 17.3 %copy.47 = bf16[2,256,2560]{1,0,2:T(2,128)(2,1)} copy(bf16[2,256,2560]{1,2,0:T(8,128)(2,1)S(1)} %bitcast.143) | data formatting | bytes 5242880 | tf_op jit(solution)/shard_map/all_to_all | solution.py:35
  75.1 4.2 %reshape.462 = bf16[512,20,128]{0,2,1:T(8,128)(2,1)S(1)} reshape(bf16[2,256,2560]{1,0,2:T(2,128)(2,1)} %copy.47) | data formatting | bytes 5242880 | tf_op jit(solution)/shard_map/reshape | solution.py:44
  79.3 2.6 copy.50
  81.9 7.9 %fusion.39 = bf16[20,512,384]{2,1,0:T(8,128)(2,1)S(1)} fusion(bf16[512,20,128]{2,0,1:T(8,128)(2,1)} %copy.50, bf16[512,20,128]{2,0,1:T(8,128)(2,1)} %copy.49, bf16[512,20,128]{2,0,1:T(8,128)(2,1)} %copy.48, s32[20,512]{1,0:T(8,128)S(1)} %broadcast_subtract_fusion), kind=kOutput, calls=%fused_computation.46 | convolution fusion | flops 4059299840 | bytes 15769600 | tf_op jit(solution)/shard_map/hit,thd->hid/dot_general | solution.py:48
  89.7 3.1 %fusion.68 = (bf16[20,512,128]{2,1,0:T(8,128)(2,1)}, bf16[20,512,128]{2,1,0:T(8,128)(2,1)S(1)}, bf16[20,512,128]{2,1,0:T(8,128)(2,1)}) fusion(bf16[20,512,384]{2,1,0:T(8,128)(2,1)S(1)} %fusion.39), kind=kLoop, calls=%fused_computation.105 | loop fusion | bytes 15728640 | tf_op jit(solution)/shard_map/slice | solution.py:52
  92.8 5.2 %reshape.467 = bf16[80,16384]{1,0:T(8,128)(2,1)} reshape(bf16[20,512,128]{2,1,0:T(8,128)(2,1)} %get-tuple-element.99) | data formatting | bytes 5242880 | tf_op jit(solution)/shard_map/reshape | solution.py:69
  98.0 3.1 %reshape.468 = bf16[80,16384]{1,0:T(8,128)(2,1)} reshape(bf16[20,512,128]{2,1,0:T(8,128)(2,1)S(1)} %get-tuple-element.100) | data formatting | bytes 5242880 | tf_op jit(solution)/shard_map/reshape | solution.py:70
  101.6 3.4 %convolution_convert_fusion.3 = bf16[16,2,32768]{2,0,1:T(8,128)(2,1)S(1)} fusion(bf16[80,16384]{1,0:T(8,128)(2,1)} %reshape.468, bf16[80,16384]{1,0:T(8,128)(2,1)} %reshape.467, s32[16,80]{1,0:T(8,128)S(1)} %sub.46, pred[16,80]{1,0:T(8,128)(4,1)S(1)} %copy.57), kind=kOutput, calls=%fused_computation.35 | convolution fusion | flops 179311616 | bytes 7346432 | tf_op jit(solution)/shard_map/scp,pw->scw/dot_general | solution.py:74
  106.4 6.4 %all-to-all-start.5 = ((bf16[16,2,128,128]{3,2,1,0:T(8,128)(2,1)}), bf16[16,2,128,128]{3,2,1,0:T(8,128)(2,1)S(1)}, u32[]{:S(2)}, u32[]{:S(2)}) async-start(bf16[16,2,128,128]{3,2,1,0:T(8,128)(2,1)} %copy.61), calls=%async_computation.5 | async-start | bytes 2097152 | tf_op jit(solution)/shard_map/all_to_all | solution.py:134
  114.1 23.1 %all-to-all-done.5 = bf16[16,2,128,128]{3,2,1,0:T(8,128)(2,1)S(1)} async-done(((bf16[16,2,128,128]{3,2,1,0:T(8,128)(2,1)}), bf16[16,2,128,128]{3,2,1,0:T(8,128)(2,1)S(1)}, u32[]{:S(2)}, u32[]{:S(2)}) %all-to-all-start.5) | async-done | bytes 1048608 | tf_op jit(solution)/shard_map/all_to_all | solution.py:134
  137.2 4.6 %all-to-all-start.4 = ((bf16[16,2,128,128]{3,2,1,0:T(8,128)(2,1)}), bf16[16,2,128,128]{3,2,1,0:T(8,128)(2,1)S(1)}, u32[]{:S(2)}, u32[]{:S(2)}) async-start(bf16[16,2,128,128]{3,2,1,0:T(8,128)(2,1)} %copy.60), calls=%async_computation.4 | async-start | bytes 2097152 | tf_op jit(solution)/shard_map/all_to_all | solution.py:133
  145.9 1.8 gather_fusion.2
  149.4 16.7 %all-to-all-done.4 = bf16[16,2,128,128]{3,2,1,0:T(8,128)(2,1)S(1)} async-done(((bf16[16,2,128,128]{3,2,1,0:T(8,128)(2,1)}), bf16[16,2,128,128]{3,2,1,0:T(8,128)(2,1)S(1)}, u32[]{:S(2)}, u32[]{:S(2)}) %all-to-all-start.4) | async-done | bytes 1048608 | tf_op jit(solution)/shard_map/all_to_all | solution.py:133
  166.8 81.6 %while.11 = (s32[]{:T(128)}, bf16[20,4,128,128]{3,2,1,0:T(8,128)(2,1)}, pred[20,4,1]{0,1,2:T(4,128)(4,1)S(1)}, bf16[20,4,128,128]{3,2,1,0:T(8,128)(2,1)}, s32[20...) while((s32[]{:T(128)}, ...), condition=%wide.region_8.9_spmd.clone, body=%wide.region_5.8_spmd.clone.sunk | while | flops 59507712 | bytes 3937973 | solution.py:148
  248.4 7.2 %convert_bitcast_fusion = bf16[512,20,128]{0,2,1:T(8,128)(2,1)} fusion(bf16[20,512,128]{2,1,0:T(8,128)(2,1)} %bitcast.160, s32[20,512]{1,0:T(8,128)S(1)} %broadcast_subtract_fusion), kind=kOutput, calls=%fused_computation.51 | convolution fusion | flops 1348730880 | bytes 5283840 | tf_op jit(solution)/shard_map/hit,hid->thd/dot_general | solution.py:150
  255.6 3.5 %all_to_all.60 = bf16[2,256,2560]{1,0,2:T(2,128)(2,1)S(1)} reshape(bf16[512,20,128]{0,2,1:T(8,128)(2,1)} %convert_bitcast_fusion) | data formatting | bytes 5242880 | tf_op jit(solution)/shard_map/all_to_all | solution.py:154
  259.5 7.9 %all_to_all.71 = bf16[2,256,2560]{1,2,0:T(8,128)(2,1)S(1)} all-to-all(bf16[2,256,2560]{1,2,0:T(8,128)(2,1)S(1)} %copy.65), channel_id=1, replica_groups=mesh['head'=2,'seq'=16] {'head'}, dimensions={0} | all-to-all | bytes 5242880 | tf_op jit(solution)/shard_map/all_to_all | solution.py:154
  267.4 2.8 %copy.66 = bf16[256,5120]{1,0:T(8,128)(2,1)} copy(bf16[256,5120]{0,1:T(8,128)(2,1)S(1)} %bitcast.146) | data formatting | bytes 5242880 | tf_op jit(solution)/shard_map/all_to_all | solution.py:154
  (217 shorter events, 92.0 us)
Async XLA Ops:
  3.6 4.7 %copy-start.1 = (s32[20,4,64]{2,1,0:T(4,128)S(1)}, s32[20,4,64]{2,1,0:T(4,128)}, u32[]{:S(2)}) copy-start(s32[20,4,64]{2,1,0:T(4,128)} %param.11) | copy-start | bytes 61444
  3.6 9.8 %all-to-all-start = ((bf16[2,256,2560]{2,1,0:T(8,128)(2,1)}), bf16[2,256,2560]{2,1,0:T(8,128)(2,1)S(1)}, u32[]{:S(2)}, u32[]{:S(2)}) async-start(bf16[2,256,2560]{2,1,0:T(8,128)(2,1)} %pad_maximum_fusion), calls=%async_computation | async-start | bytes 5242880 | tf_op jit(solution)/shard_map/all_to_all | solution.py:14
  13.4 1.5 copy-start
  14.9 15.7 %all-to-all-start.1 = ((bf16[256,2,2560]{0,2,1:T(8,128)(2,1)}), bf16[256,2,2560]{0,2,1:T(8,128)(2,1)}, u32[]{:S(2)}, u32[]{:S(2)}) async-start(bf16[256,2,2560]{0,2,1:T(8,128)(2,1)} %bitcast.144), calls=%async_computation.1 | async-start | bytes 5242880 | tf_op jit(solution)/shard_map/all_to_all | solution.py:34
  30.6 20.6 %all-to-all-start.2 = ((bf16[256,2,2560]{0,2,1:T(8,128)(2,1)}), bf16[256,2,2560]{0,2,1:T(8,128)(2,1)S(1)}, u32[]{:S(2)}, u32[]{:S(2)}) async-start(bf16[256,2,2560]{0,2,1:T(8,128)(2,1)} %bitcast.145), calls=%async_computation.2 | async-start | bytes 5242880 | tf_op jit(solution)/shard_map/all_to_all | solution.py:35
  51.2 49.9 %all-to-all-start.3 = ((s32[20,16,4]{0,2,1:T(4,128)}), s32[20,16,4]{0,2,1:T(4,128)S(1)}, u32[]{:S(2)}, u32[]{:S(2)}) async-start(s32[20,16,4]{0,2,1:T(4,128)} %bitcast.11), calls=%async_computation.3 | async-start | bytes 65536 | tf_op jit(solution)/shard_map/all_to_all | solution.py:56
  79.3 2.6 copy-start.2
  106.4 30.7 %all-to-all-start.5 = ((bf16[16,2,128,128]{3,2,1,0:T(8,128)(2,1)}), bf16[16,2,128,128]{3,2,1,0:T(8,128)(2,1)S(1)}, u32[]{:S(2)}, u32[]{:S(2)}) async-start(bf16[16,2,128,128]{3,2,1,0:T(8,128)(2,1)} %copy.61), calls=%async_computation.5 | async-start | bytes 2097152 | tf_op jit(solution)/shard_map/all_to_all | solution.py:134
  137.2 28.9 %all-to-all-start.4 = ((bf16[16,2,128,128]{3,2,1,0:T(8,128)(2,1)}), bf16[16,2,128,128]{3,2,1,0:T(8,128)(2,1)S(1)}, u32[]{:S(2)}, u32[]{:S(2)}) async-start(bf16[16,2,128,128]{3,2,1,0:T(8,128)(2,1)} %copy.60), calls=%async_computation.4 | async-start | bytes 2097152 | tf_op jit(solution)/shard_map/all_to_all | solution.py:133
